TPU v7x, 512 devices: a whole 4x4x16 slice. The times are simulated.
512 devices in a mesh: space: 32 (over y, x, core), blk: 16 (over z).
Axes of the slice: x: 4, y: 4, z: 16, core: 2. Of those that a mesh axis runs over, the one named last changes fastest.
Arguments:
- snapshots: bfloat16 [20480, 16384], P('blk', 'space'), may hold values from -6 to 6
- row_scales: float32 [20480], P('blk'), may hold values from 0.3 to 3
- block_offsets: int32 [64], P('blk'), may hold values from 0 to 768, as said below
- freq_index: int32 [16], replicated, may hold values from 1 to 255
Outputs:
- modes: float32 [16, 16384, 128], P('blk', 'space')
- r_factor: float32 [16, 2, 64, 64], P('blk')
Inputs may be any that keep to these rules, and one draw needn't show every extreme that they name: `block_offsets`: block offsets index the snapshots held by the block's own index of blk; within every group of 4 blocks they are distinct and increasing, block i of a group lies between i * 256 - 512 / 4 and i * 256 + 512 / 4; in the first group the first is 0 and the last is 768.
All inputs are finite; a program needn't handle non-finite values.
Results may differ from a plain program's by a relative error of at most 0.0064.
Values may be sent and summed in bfloat16 or wider, within the bound.
A program may use at most 64 MiB of HBM per device.

v0:
```python
import math
import jax
import jax.numpy as jnp
from jax import lax
from jax.sharding import PartitionSpec as P

NFFT = 512


def padded_coeffs(row_scales, block_offsets, freq_index):
    rows = row_scales.shape[0]
    times = jnp.arange(rows, dtype=jnp.int32)[None, :] - block_offsets[:, None]
    inside = (times >= 0) & (times < NFFT)
    hann = 0.5 - 0.5 * jnp.cos(2.0 * math.pi / NFFT * times.astype(jnp.float32))
    weight = jnp.where(inside, hann * row_scales[None, :], 0.0) / math.sqrt(NFFT)
    quarter = jnp.arange(2, dtype=jnp.int32) * (NFFT // 4)
    phase = freq_index[:, None, None, None] * times[None, :, None, :]
    phase = phase + quarter[None, None, :, None] & NFFT - 1
    table = jnp.cos(2.0 * math.pi / NFFT * phase.astype(jnp.float32))
    return (table * weight[None, :, None, :]).astype(jnp.bfloat16)


def local(snapshots, row_scales, block_offsets, freq_index):
    points_here = snapshots.shape[1]
    freq_count = freq_index.shape[0]
    blocks_here = block_offsets.shape[0]
    coeffs = padded_coeffs(row_scales, block_offsets, freq_index)
    coeffs = coeffs.reshape(freq_count * blocks_here * 2, -1)
    spectra = jnp.dot(coeffs, snapshots, preferred_element_type=jnp.float32)
    spectra = spectra.astype(jnp.bfloat16).reshape(freq_count, 2 * blocks_here, points_here)
    regrouped = lax.all_to_all(spectra, "blk", split_axis=0, concat_axis=1, tiled=True)
    rows = regrouped[0]
    total_points = points_here * lax.axis_size("space")
    product = jnp.dot(rows, rows.T, preferred_element_type=jnp.float32) / total_points
    product = lax.optimization_barrier(lax.psum(product, "space"))
    width = product.shape[0]
    quads = product.reshape(width // 2, 2, width // 2, 2)
    real = quads[:, 0, :, 0] + quads[:, 1, :, 1]
    imag = quads[:, 0, :, 1] - quads[:, 1, :, 0]
    gram = jnp.stack([jnp.stack([real, imag], -1), jnp.stack([-imag, real], -1)], 1).reshape(
        width, width
    )
    lower = jnp.linalg.cholesky(gram)
    identity = jnp.eye(width, dtype=jnp.float32)
    inverse_lower = jax.scipy.linalg.solve_triangular(lower, identity, lower=True)
    modes = lax.dot_general(
        rows.astype(jnp.float32),
        inverse_lower,
        (((0,), (1,)), ((), ())),
        precision=lax.Precision.HIGHEST,
    )
    upper = lower.T
    r_factor = jnp.stack([upper[0::2, 0::2], upper[0::2, 1::2]], 0)
    return (modes[None], r_factor[None])


def solution(mesh):
    return jax.shard_map(
        local,
        mesh=mesh,
        in_specs=(P("blk", "space"), P("blk"), P("blk"), P()),
        out_specs=(P("blk", "space", None), P("blk", None, None, None)),
        check_vma=False,
    )
```

profile of v0, /device:TPU:1, one launch (start us, length us, event | category | flops | bytes accessed | tf_op | source)
XLA Modules:
  0.0 218.7 jit_solution(5565477457189449705)
XLA Ops:
  7.2 0.8 iota_subtract_fusion
  8.1 0.9 select_multiply_fusion
  9.1 0.8 broadcast_multiply_fusion
  9.9 0.2 add.47
  10.2 0.5 add.48
  10.6 0.2 mul.83
  10.8 0.5 mul.84
  11.3 2.6 %fusion.2 = bf16[16,8,512]{2,1,0:T(8,128)(2,1)S(1)} fusion(bf16[1280,512]{1,0:T(8,128)(2,1)S(1)} %copy-done, f32[128,1280]{1,0:T(8,128)S(1)} %mul.84, s32[128,1280]{1,0:T(8,128)S(1)} %add.48, s32[128]{0:T(128)S(1)} %add.50), kind=kOutput, calls=%fused_computation.6 | convolution fusion | flops 168820736 | bytes 2753024 | tf_op jit(solution)/shard_map/dot_general | solution.py:29
  13.9 27.5 %all_to_all.4 = bf16[16,8,512]{2,1,0:T(8,128)(2,1)S(1)} all-to-all(bf16[16,8,512]{2,1,0:T(8,128)(2,1)S(1)} %fusion.2), channel_id=1, replica_groups=mesh['space'=32,'blk'=16] {'blk'}, dimensions={0} | all-to-all | bytes 262144 | tf_op jit(solution)/shard_map/all_to_all | solution.py:31
  41.4 0.8 convolution_multiply_fusion
  42.2 124.5 %all-reduce.2.cloned.1.call-done = f32[128,128]{1,0:T(8,128)} async-done(((f32[128,128]{1,0:T(8,128)}), f32[128,128]{1,0:T(8,128)}) %all-reduce.2.cloned.1.call-update) | async-done | bytes 65552 | tf_op jit(solution)/shard_map/psum | solution.py:35
  166.7 6.2 %reshape.147 = f32[64,2,64,2]{3,2,1,0:T(8,128)} reshape(f32[128,128]{1,0:T(8,128)} %all-reduce.2.cloned.1.call-done) | data formatting | bytes 131072 | tf_op jit(solution)/shard_map/reshape | solution.py:37
  173.0 5.7 %fusion = (f32[64,64]{1,0:T(8,128)S(1)}, f32[64,64]{1,0:T(8,128)S(1)}) fusion(f32[64,2,64,2]{3,2,1,0:T(8,128)} %reshape.147), kind=kLoop, calls=%fused_computation.1 | loop fusion | flops 8192 | bytes 98304 | tf_op jit(solution)/shard_map/sub | solution.py:39
  178.8 2.7 %copy.21 = f32[64,2,64,2]{3,2,1,0:T(8,128)} copy(f32[64,2,64,2]{2,0,3,1:T(8,128)S(1)} %pad_maximum_fusion) | data formatting | bytes 131072 | tf_op jit(solution)/shard_map/stack | solution.py:40
  181.5 4.2 %reshape.148 = f32[128,128]{1,0:T(8,128)S(1)} reshape(f32[64,2,64,2]{3,2,1,0:T(8,128)} %copy.21) | data formatting | bytes 131072 | tf_op jit(solution)/shard_map/reshape | solution.py:40
  185.8 11.7 %cholesky.17 = f32[128,128]{1,0:T(8,128)S(1)} custom-call(f32[128,128]{1,0:T(8,128)S(1)} %fusion.10), custom_call_target="Cholesky" | custom-call | tf_op jit(solution)/shard_map/jit(cholesky)/cholesky | solution.py:43
  197.5 0.6 compare_reduce_fusion
  198.2 0.7 fusion.11
  198.8 0.6 slice.35
  199.4 0.6 slice.34
  200.0 9.8 %custom-call.7 = f32[1,128,128]{1,2,0:T(8,128)S(1)} custom-call(f32[1,128,128]{2,1,0:T(8,128)S(1)} %get-tuple-element.13), custom_call_target="InvertDiagBlocksLowerTriangular" | custom-call | tf_op jit(solution)/shard_map/jit(_solve_triangular)/triangular_solve | solution.py:45
  209.9 0.2 fusion.8
  210.1 0.7 copy.23
  210.8 1.0 convolution_bitcast_fusion
  (14 shorter events, 0.4 us)
Async XLA Ops:
  7.2 4.1 %copy-start = (bf16[1280,512]{1,0:T(8,128)(2,1)S(1)}, bf16[1280,512]{1,0:T(8,128)(2,1)}, u32[]{:S(2)}) copy-start(bf16[1280,512]{1,0:T(8,128)(2,1)} %param.4) | copy-start | bytes 3932164
  7.2 159.5 %all-reduce.2.cloned.1.call-start = ((), (), s32[]{:S(2)}) async-start(), calls=%async_computation.1 | async-start | bytes 131072 | tf_op jit(solution)/shard_map/psum | solution.py:35
Sparse Core Ops, SparseCore 0:
  42.3 124.3 all-reduce.1
where the time goes:
time: 219 us
  waiting for transfers between devices  125 us (57%)
  other arithmetic  31.2 us (14%)
  blocking collectives  27.5 us (13%)
  local copies, waits for them, and re-layouts  16.6 us (8%)
  between operations  14.2 us (6%)
  matrix products  4.68 us (2%)
    psum x1, waiting for transfers between devices, local(): product = lax.optimization_barrier(lax.psum(product, 'space'))  124 us
    all_to_all x1, blocking collectives, local(): lax.all_to_all(spectra, 'blk', split_axis=0, concat_axis=1, tiled=True)  27.5 us
    another operation x3, other arithmetic, local(): lower = jnp.linalg.cholesky(gram)  12.4 us
    another operation x1, other arithmetic, local(): jax.scipy.linalg.solve_triangular(lower, identity, lower=True)  9.81 us
    reshape x1, local copies, waits for them, and re-layouts, local(): quads = product.reshape(width // 2, 2, width // 2, 2)  6.24 us
    sub x1, other arithmetic, local(): imag = quads[:, 0, :, 1] - quads[:, 1, :, 0]  5.74 us
  transfers between devices with their start and end apart: 1, of which 1 were waited for; matrix products, arithmetic and copies ran while one was open for 0% of the time, Pallas kernels for 0%

commit v1 on v0

--- a/solution.py
+++ b/solution.py
@@ -32,7 +32,7 @@
     rows = regrouped[0]
     total_points = points_here * lax.axis_size("space")
     product = jnp.dot(rows, rows.T, preferred_element_type=jnp.float32) / total_points
-    product = lax.optimization_barrier(lax.psum(product, "space"))
+    product = lax.optimization_barrier(jnp.sum(lax.all_gather(product, "space"), axis=0))
     width = product.shape[0]
     quads = product.reshape(width // 2, 2, width // 2, 2)
     real = quads[:, 0, :, 0] + quads[:, 1, :, 1]

time: 219 us -> 151 us (0.69)
  waiting for transfers between devices: 125 us -> 55.6 us
    psum x1 -> x0, waiting for transfers between devices: 124 us -> none  [local(): product = lax.optimization_barrier(lax.psum(product, 'space'))]
    all_gather x0 -> x1, waiting for transfers between devices: none -> 55.5 us  [local(): lax.all_gather(product, 'space')]
where the time goes in v1:
time: 151 us
  waiting for transfers between devices  55.6 us (37%)
  other arithmetic  32.9 us (22%)
  blocking collectives  27.5 us (18%)
  local copies, waits for them, and re-layouts  15.9 us (11%)
  between operations  14.2 us (9%)
  matrix products  4.68 us (3%)
    all_gather x1, waiting for transfers between devices, local(): lax.all_gather(product, 'space')  55.5 us
    all_to_all x1, blocking collectives, local(): lax.all_to_all(spectra, 'blk', split_axis=0, concat_axis=1, tiled=True)  27.5 us
    another operation x3, other arithmetic, local(): lower = jnp.linalg.cholesky(gram)  12.4 us
    another operation x1, other arithmetic, local(): jax.scipy.linalg.solve_triangular(lower, identity, lower=True)  9.81 us
    sub x1, other arithmetic, local(): imag = quads[:, 0, :, 1] - quads[:, 1, :, 0]  5.74 us
    reshape x1, local copies, waits for them, and re-layouts, local(): quads = product.reshape(width // 2, 2, width // 2, 2)  5.5 us
    reshape x2, local copies, waits for them, and re-layouts, local(): jnp.stack([jnp.stack([real, imag], -1), jnp.stack([-imag, real], -1)], 1)  4.27 us
  transfers between devices with their start and end apart: 1, of which 1 were waited for; matrix products, arithmetic and copies ran while one was open for 0% of the time, Pallas kernels for 0%

profile of v1, /device:TPU:1, one launch (start us, length us, event | category | flops | bytes accessed | tf_op | source)
XLA Modules:
  0.0 150.7 jit_solution(17473127131661264827)
XLA Ops:
  7.2 0.8 iota_subtract_fusion
  8.1 0.9 select_multiply_fusion
  9.1 0.8 broadcast_multiply_fusion
  9.9 0.2 add.45
  10.2 0.5 add.46
  10.8 0.5 mul.84
  11.3 2.6 %fusion.2 = bf16[16,8,512]{2,1,0:T(8,128)(2,1)S(1)} fusion(bf16[1280,512]{1,0:T(8,128)(2,1)S(1)} %copy-done, f32[128,1280]{1,0:T(8,128)S(1)} %mul.84, s32[128,1280]{1,0:T(8,128)S(1)} %add.46, s32[128]{0:T(128)S(1)} %add.48), kind=kOutput, calls=%fused_computation.6 | convolution fusion | flops 168820736 | bytes 2753024 | tf_op jit(solution)/shard_map/dot_general | solution.py:29
  13.9 27.5 %all_to_all.4 = bf16[16,8,512]{2,1,0:T(8,128)(2,1)S(1)} all-to-all(bf16[16,8,512]{2,1,0:T(8,128)(2,1)S(1)} %fusion.2), channel_id=1, replica_groups=mesh['space'=32,'blk'=16] {'blk'}, dimensions={0} | all-to-all | bytes 262144 | tf_op jit(solution)/shard_map/all_to_all | solution.py:31
  41.4 0.8 convolution_multiply_fusion
  42.2 55.5 %all-gather.3.cloned.1.call-done = f32[4096,128]{1,0:T(8,128)} async-done(((f32[128,128]{1,0:T(8,128)}), f32[4096,128]{1,0:T(8,128)}) %all-gather.3.cloned.1.call-update) | async-done | bytes 2097168 | tf_op jit(solution)/shard_map/all_gather | solution.py:35
  97.8 1.7 %reduce_sum.9 = f32[128,128]{1,0:T(8,128)S(1)} reduce(f32[32,128,128]{2,1,0:T(8,128)} %bitcast.36, f32[]{:T(128)} %constant.57.clone.1), dimensions={0}, to_apply=%region_0.1 | reduce | flops 507904 | bytes 2162692 | tf_op jit(solution)/shard_map/reduce_sum | solution.py:35
  99.5 5.5 %reshape.147 = f32[64,2,64,2]{3,2,1,0:T(8,128)} reshape(f32[128,128]{1,0:T(8,128)S(1)} %reduce_sum.9) | data formatting | bytes 131072 | tf_op jit(solution)/shard_map/reshape | solution.py:37
  105.0 5.7 %fusion = (f32[64,64]{1,0:T(8,128)S(1)}, f32[64,64]{1,0:T(8,128)S(1)}) fusion(f32[64,2,64,2]{3,2,1,0:T(8,128)} %reshape.147), kind=kLoop, calls=%fused_computation.1 | loop fusion | flops 8192 | bytes 98304 | tf_op jit(solution)/shard_map/sub | solution.py:39
  110.8 2.7 %copy.17 = f32[64,2,64,2]{3,2,1,0:T(8,128)} copy(f32[64,2,64,2]{2,0,3,1:T(8,128)S(1)} %pad_maximum_fusion) | data formatting | bytes 131072 | tf_op jit(solution)/shard_map/stack | solution.py:40
  113.5 4.2 %reshape.148 = f32[128,128]{1,0:T(8,128)S(1)} reshape(f32[64,2,64,2]{3,2,1,0:T(8,128)} %copy.17) | data formatting | bytes 131072 | tf_op jit(solution)/shard_map/reshape | solution.py:40
  117.8 11.7 %cholesky.17 = f32[128,128]{1,0:T(8,128)S(1)} custom-call(f32[128,128]{1,0:T(8,128)S(1)} %fusion.10), custom_call_target="Cholesky" | custom-call | tf_op jit(solution)/shard_map/jit(cholesky)/cholesky | solution.py:43
  129.5 0.6 compare_reduce_fusion
  130.2 0.7 fusion.11
  130.8 0.6 slice.35
  131.4 0.6 slice.34
  132.1 9.8 %custom-call.7 = f32[1,128,128]{1,2,0:T(8,128)S(1)} custom-call(f32[1,128,128]{2,1,0:T(8,128)S(1)} %get-tuple-element.13), custom_call_target="InvertDiagBlocksLowerTriangular" | custom-call | tf_op jit(solution)/shard_map/jit(_solve_triangular)/triangular_solve | solution.py:45
  141.9 0.2 fusion.8
  142.1 0.7 copy.19
  142.8 1.0 convolution_bitcast_fusion
  (15 shorter events, 0.6 us)
Async XLA Ops:
  7.2 4.1 %copy-start = (bf16[1280,512]{1,0:T(8,128)(2,1)S(1)}, bf16[1280,512]{1,0:T(8,128)(2,1)}, u32[]{:S(2)}) copy-start(bf16[1280,512]{1,0:T(8,128)(2,1)} %param.4) | copy-start | bytes 3932164
  7.2 90.6 %all-gather.3.cloned.1.call-start = ((), (), s32[]{:S(2)}) async-start(), calls=%async_computation.1 | async-start | bytes 2162688 | tf_op jit(solution)/shard_map/all_gather | solution.py:35
Sparse Core Ops, SparseCore 0:
  42.3 55.3 all-gather.2
